TPU v7x, 512 devices: a whole 4x4x16 slice. The times are simulated.
512 devices in a mesh: row: 16 (over z_lo, y), col: 32 (over x, z_hi, core).
Axes of the slice: x: 4, y: 4, z: 16 (z_hi: 4, z_lo: 4; z = z_hi * 4 + z_lo), core: 2. Of those that a mesh axis runs over, the one named last changes fastest.
Arguments:
- tiles: bfloat16 [16, 32, 32, 128, 128], P('row', 'col'), may hold values from -0.5 to 0.5
- tile_slots: int32 [16, 32, 32], P('row', 'col'), may hold values from 0 to 191, as said below
- tile_counts: int32 [16, 32], P('row', 'col'), may hold values from 8 to 32, as said below
- user_degree: int32 [32768], P('row'), may hold values from 1 to 64
- item_degree: int32 [49152], P('col'), may hold values from 1 to 64
- start_panel: float32 [64, 49152], P(None, ('col', 'row')), may hold values from -6 to 6
Outputs:
- left_panel: float32 [64, 32768], P(None, ('row', 'col'))
- right_panel: float32 [64, 49152], P(None, ('col', 'row'))
- left_factors: float32 [3, 64, 64], replicated
- right_factors: float32 [3, 64, 64], replicated
Inputs may be any that keep to these rules, and one draw needn't show every extreme that they name: `tile_slots`: within one grid cell the 32 slot numbers are distinct; slot s is local tile row s // 12 and local tile column s % 12; entries from position tile_counts on are padding. `tile_counts`: some grid cell holds 32 live tiles.
All inputs are finite; a program needn't handle non-finite values.
Results may differ from a plain program's by a relative error of at most 0.0005.
Values sent between devices are 32-bit elements; how exact they have to be, the bound alone decides.
No kernel may reach another device: no remote copies, remote signals or barrier semaphores. Data moves between devices by JAX's collectives and lax.ppermute only.
A program may use at most 64 MiB of HBM per device.

v0:
```python
import math
import jax
import jax.numpy as jnp
from jax import lax
from jax.sharding import PartitionSpec as P

STEPS = 3
HIGH = lax.Precision.HIGHEST


def gram_of(vectors):
    return jnp.einsum("bn,cn->bc", vectors, vectors, precision=HIGH)


def solve_lower(factor, vectors):
    return lax.linalg.triangular_solve(factor, vectors, left_side=True, lower=True)


def per_device(tiles, tile_slots, tile_counts, user_degree, item_degree, start_panel):
    tile_stack = tiles[0, 0].astype(jnp.float32)
    slot_list = tile_slots[0, 0]
    tile_total = tile_counts[0, 0]
    slot_count = tile_stack.shape[0]
    tile_width = tile_stack.shape[1]
    row_blocks = user_degree.shape[0] // tile_width
    col_blocks = item_degree.shape[0] // tile_width
    block_width = start_panel.shape[0]
    live_mask = jnp.arange(slot_count) < tile_total
    local_rows = slot_list // col_blocks
    local_cols = slot_list % col_blocks
    row_select = (
        (local_rows[:, None] == jnp.arange(row_blocks)[None, :]) & live_mask[:, None]
    ).astype(jnp.float32)
    col_select = (
        (local_cols[:, None] == jnp.arange(col_blocks)[None, :]) & live_mask[:, None]
    ).astype(jnp.float32)
    user_scale = lax.rsqrt(user_degree.astype(jnp.float32))
    item_scale = lax.rsqrt(item_degree.astype(jnp.float32))
    user_group = row_blocks * tile_width // lax.axis_size("col")
    item_group = col_blocks * tile_width // lax.axis_size("row")
    user_offset = lax.axis_index("col") * user_group
    item_offset = lax.axis_index("row") * item_group
    user_scale_own = lax.dynamic_slice_in_dim(user_scale, user_offset, user_group)
    item_scale_own = lax.dynamic_slice_in_dim(item_scale, item_offset, item_group)
    start_total = lax.psum(gram_of(start_panel), ("row", "col"))
    start_factor = jnp.linalg.cholesky(start_total)
    item_basis = solve_lower(start_factor, start_panel)
    user_basis = start_panel[:, :0]
    item_factor = start_factor
    user_list = []
    item_list = []
    for iteration in range(STEPS):
        scaled = item_basis * item_scale_own[None, :]
        item_full = lax.all_gather(scaled, "row", axis=1, tiled=True)
        forward_panel_blocks = item_full.reshape(block_width, col_blocks, tile_width)
        forward_chosen = jnp.take(forward_panel_blocks, local_cols, axis=1)
        forward_partial_value = jnp.einsum(
            "mrc,bmc->bmr", tile_stack, forward_chosen, precision=HIGH
        )
        forward_summed = jnp.einsum(
            "bmr,mk->bkr", forward_partial_value, row_select, precision=HIGH
        )
        forward = (
            lax.psum_scatter(
                forward_summed.reshape(block_width, row_blocks * tile_width),
                "col",
                scatter_dimension=1,
                tiled=True,
            )
            * user_scale_own[None, :]
        )
        if iteration > 0:
            forward = forward - jnp.dot(item_factor.T, user_basis, precision=HIGH)
        user_factor = jnp.linalg.cholesky(lax.psum(gram_of(forward), ("row", "col")))
        user_basis = solve_lower(user_factor, forward)
        scaled = user_basis * user_scale_own[None, :]
        user_full = lax.all_gather(scaled, "col", axis=1, tiled=True)
        panel_blocks = user_full.reshape(block_width, row_blocks, tile_width)
        chosen = jnp.take(panel_blocks, local_rows, axis=1)
        partial_value = jnp.einsum("mrc,bmr->bmc", tile_stack, chosen, precision=HIGH)
        summed = jnp.einsum("bmc,mk->bkc", partial_value, col_select, precision=HIGH)
        backward = (
            lax.psum_scatter(
                summed.reshape(block_width, col_blocks * tile_width),
                "row",
                scatter_dimension=1,
                tiled=True,
            )
            * item_scale_own[None, :]
        )
        backward = backward - jnp.dot(user_factor.T, item_basis, precision=HIGH)
        item_factor = jnp.linalg.cholesky(lax.psum(gram_of(backward), ("row", "col")))
        item_basis = solve_lower(item_factor, backward)
        user_list.append(user_factor)
        item_list.append(item_factor)
    user_total = row_blocks * tile_width * lax.axis_size("row")
    item_total = col_blocks * tile_width * lax.axis_size("col")
    return (
        math.sqrt(user_total) * user_basis,
        math.sqrt(item_total) * item_basis,
        jnp.stack(user_list),
        jnp.stack(item_list),
    )


def solution(mesh):
    in_specs = (
        P("row", "col", None, None, None),
        P("row", "col", None),
        P("row", "col"),
        P("row"),
        P("col"),
        P(None, ("col", "row")),
    )
    out_specs = (P(None, ("row", "col")), P(None, ("col", "row")), P(), P())
    return jax.shard_map(
        per_device, mesh=mesh, in_specs=in_specs, out_specs=out_specs, check_vma=False
    )
```

profile of v0, /device:TPU:1, one launch (start us, length us, event | category | flops | bytes accessed | tf_op | source)
XLA Modules:
  0.0 1727.9 jit_solution(9248479124465914468)
XLA Ops:
  9.7 111.2 %psum.49 = f32[64,64]{0,1:T(8,128)S(1)} all-reduce(f32[64,64]{0,1:T(8,128)S(1)} %fusion.153), channel_id=1, replica_groups=mesh['row'=16,'col'=32] {'row','col'}, use_global_device_ids=true, to_apply=%region_0.1 | all-reduce | flops 4096 | bytes 32768 | tf_op jit(solution)/shard_map/psum | solution.py:45
  120.9 5.8 cholesky.119
  128.1 4.9 custom-call.13
  134.1 33.8 %all-gather = f32[16,96,64]{1,2,0:T(8,128)S(1)} all-gather(f32[1,96,64]{1,2,0:T(8,128)S(1)} %multiply_bitcast_fusion.2), channel_id=1, replica_groups=mesh['row'=16,'col'=32] {'row'}, dimensions={0}, use_global_device_ids=true | all-gather | bytes 417792 | tf_op jit(solution)/shard_map/all_gather | solution.py:54
  174.6 110.4 %reduce-scatter.19.cloned.1.call-done = f32[64,64]{1,0:T(8,128)} async-done(((f32[2048,64]{1,0:T(8,128)}), f32[64,64]{1,0:T(8,128)}) %reduce-scatter.19.cloned.1.call-update) | async-done | bytes 16400
  286.0 101.8 %psum.50 = f32[64,64]{0,1:T(8,128)S(1)} all-reduce(f32[64,64]{0,1:T(8,128)S(1)} %fusion.81), channel_id=1, replica_groups=mesh['row'=16,'col'=32] {'row','col'}, use_global_device_ids=true, to_apply=%region_4.8 | all-reduce | flops 4096 | bytes 32768 | tf_op jit(solution)/shard_map/psum | solution.py:74
  388.0 5.8 cholesky.130
  395.1 4.9 custom-call.14
  400.4 57.0 %all_gather.19 = f32[64,2048]{0,1:T(8,128)S(1)} all-gather(f32[64,64]{0,1:T(8,128)S(1)} %copy.109), channel_id=1, replica_groups=mesh['row'=16,'col'=32] {'col'}, dimensions={1}, use_global_device_ids=true | all-gather | bytes 540672 | tf_op jit(solution)/shard_map/all_gather | solution.py:77
  461.6 71.2 %reduce-scatter.21.cloned.1.call-done = f32[96,64]{1,0:T(8,128)} async-done(((f32[1536,64]{1,0:T(8,128)}), f32[96,64]{1,0:T(8,128)}) %reduce-scatter.21.cloned.1.call-update) | async-done | bytes 24592
  534.8 112.8 %psum.51 = f32[64,64]{0,1:T(8,128)S(1)} all-reduce(f32[64,64]{0,1:T(8,128)S(1)} %fusion.154), channel_id=1, replica_groups=mesh['row'=16,'col'=32] {'row','col'}, use_global_device_ids=true, to_apply=%region_6.12 | all-reduce | flops 4096 | bytes 32768 | tf_op jit(solution)/shard_map/psum | solution.py:92
  647.7 5.8 cholesky.141
  654.9 4.9 custom-call.15
  660.0 36.4 %all-gather.1 = f32[16,96,64]{1,2,0:T(8,128)S(1)} all-gather(f32[1,96,64]{1,2,0:T(8,128)S(1)} %multiply_bitcast_fusion.1), channel_id=1, replica_groups=mesh['row'=16,'col'=32] {'row'}, dimensions={0}, use_global_device_ids=true | all-gather | bytes 417792 | tf_op jit(solution)/shard_map/all_gather | solution.py:54
  702.3 110.1 %reduce-scatter.23.cloned.1.call-done = f32[64,64]{1,0:T(8,128)} async-done(((f32[2048,64]{1,0:T(8,128)}), f32[64,64]{1,0:T(8,128)}) %reduce-scatter.23.cloned.1.call-update) | async-done | bytes 16400
  814.3 102.0 %psum.52 = f32[64,64]{0,1:T(8,128)S(1)} all-reduce(f32[64,64]{0,1:T(8,128)S(1)} %fusion.155), channel_id=1, replica_groups=mesh['row'=16,'col'=32] {'row','col'}, use_global_device_ids=true, to_apply=%region_8.14 | all-reduce | flops 4096 | bytes 32768 | tf_op jit(solution)/shard_map/psum | solution.py:74
  916.4 5.8 cholesky.152
  923.6 4.9 custom-call.16
  928.9 56.4 %all_gather.21 = f32[64,2048]{0,1:T(8,128)S(1)} all-gather(f32[64,64]{0,1:T(8,128)S(1)} %copy.120), channel_id=1, replica_groups=mesh['row'=16,'col'=32] {'col'}, dimensions={1}, use_global_device_ids=true | all-gather | bytes 540672 | tf_op jit(solution)/shard_map/all_gather | solution.py:77
  989.6 70.9 %reduce-scatter.25.cloned.1.call-done = f32[96,64]{1,0:T(8,128)} async-done(((f32[1536,64]{1,0:T(8,128)}), f32[96,64]{1,0:T(8,128)}) %reduce-scatter.25.cloned.1.call-update) | async-done | bytes 24592
  1062.5 113.1 %psum.53 = f32[64,64]{0,1:T(8,128)S(1)} all-reduce(f32[64,64]{0,1:T(8,128)S(1)} %fusion.156), channel_id=1, replica_groups=mesh['row'=16,'col'=32] {'row','col'}, use_global_device_ids=true, to_apply=%region_10.16 | all-reduce | flops 4096 | bytes 32768 | tf_op jit(solution)/shard_map/psum | solution.py:92
  1175.6 5.8 cholesky.163
  1182.8 4.9 custom-call.17
  1188.0 36.7 %all-gather.2 = f32[16,96,64]{1,2,0:T(8,128)S(1)} all-gather(f32[1,96,64]{1,2,0:T(8,128)S(1)} %multiply_bitcast_fusion), channel_id=1, replica_groups=mesh['row'=16,'col'=32] {'row'}, dimensions={0}, use_global_device_ids=true | all-gather | bytes 417792 | tf_op jit(solution)/shard_map/all_gather | solution.py:54
  1230.5 110.1 %reduce-scatter.27.cloned.1.call-done = f32[64,64]{1,0:T(8,128)} async-done(((f32[2048,64]{1,0:T(8,128)}), f32[64,64]{1,0:T(8,128)}) %reduce-scatter.27.cloned.1.call-update) | async-done | bytes 16400
  1342.5 101.8 %psum.54 = f32[64,64]{0,1:T(8,128)S(1)} all-reduce(f32[64,64]{0,1:T(8,128)S(1)} %fusion.157), channel_id=1, replica_groups=mesh['row'=16,'col'=32] {'row','col'}, use_global_device_ids=true, to_apply=%region_12.18 | all-reduce | flops 4096 | bytes 32768 | tf_op jit(solution)/shard_map/psum | solution.py:74
  1444.4 5.8 cholesky.174
  1451.6 4.9 custom-call.18
  1457.5 56.3 %all_gather.23 = f32[64,2048]{0,1:T(8,128)S(1)} all-gather(f32[64,64]{0,1:T(8,128)S(1)} %copy.131), channel_id=1, replica_groups=mesh['row'=16,'col'=32] {'col'}, dimensions={1}, use_global_device_ids=true | all-gather | bytes 540672 | tf_op jit(solution)/shard_map/all_gather | solution.py:77
  1518.7 73.4 %reduce-scatter.29.cloned.1.call-done = f32[96,64]{1,0:T(8,128)} async-done(((f32[1536,64]{1,0:T(8,128)}), f32[96,64]{1,0:T(8,128)}) %reduce-scatter.29.cloned.1.call-update) | async-done | bytes 24592
  1594.0 113.0 %psum.55 = f32[64,64]{0,1:T(8,128)S(1)} all-reduce(f32[64,64]{0,1:T(8,128)S(1)} %fusion.158), channel_id=1, replica_groups=mesh['row'=16,'col'=32] {'row','col'}, use_global_device_ids=true, to_apply=%region_14.20 | all-reduce | flops 4096 | bytes 32768 | tf_op jit(solution)/shard_map/psum | solution.py:92
  1707.1 5.8 cholesky.185
  (130 shorter events, 63.5 us)
Async XLA Ops:
  7.2 161.9 %copy-start = (bf16[1,1,32,128,128]{4,3,2,1,0:T(8,128)(2,1)S(1)}, bf16[1,1,32,128,128]{4,3,2,1,0:T(8,128)(2,1)}, u32[]{:S(2)}) copy-start(bf16[1,1,32,128,128]{4,3,2,1,0:T(8,128)(2,1)} %param.15) | copy-start | bytes 3145732
  7.2 277.8 %reduce-scatter.19.cloned.1.call-start = ((), (), s32[]{:S(2)}) async-start(), calls=%async_computation.6 | async-start | bytes 1081344
  8.0 0.7 copy-start.2
  127.5 5.6 copy-start.1
  173.7 359.1 %reduce-scatter.21.cloned.1.call-start = ((), (), s32[]{:S(2)}) async-start(), calls=%async_computation.7 | async-start | bytes 835584
  461.6 350.8 %reduce-scatter.23.cloned.1.call-start = ((), (), s32[]{:S(2)}) async-start(), calls=%async_computation.8 | async-start | bytes 1081344
  702.3 358.2 %reduce-scatter.25.cloned.1.call-start = ((), (), s32[]{:S(2)}) async-start(), calls=%async_computation.9 | async-start | bytes 835584
  989.5 351.1 %reduce-scatter.27.cloned.1.call-start = ((), (), s32[]{:S(2)}) async-start(), calls=%async_computation.10 | async-start | bytes 1081344
  1230.5 361.6 %reduce-scatter.29.cloned.1.call-start = ((), (), s32[]{:S(2)}) async-start(), calls=%async_computation.11 | async-start | bytes 835584
Sparse Core Ops, SparseCore 0:
  173.9 111.0 reduce-scatter.18
  461.7 71.0 reduce-scatter.20
  702.4 109.9 reduce-scatter.22
  989.6 70.8 reduce-scatter.24
  1230.6 109.9 reduce-scatter.26
  1518.1 73.8 reduce-scatter.28
where the time goes:
time: 1740 us; the launch traced here: 1730 us
  blocking collectives  1030 us (59%)
  waiting for transfers between devices  546 us (31%)
  other arithmetic  87.5 us (5%)
  matrix products  25.6 us (1%)
  local copies, waits for them, and re-layouts  20.4 us (1%)
    unnamed x12, waiting for transfers between devices  546 us
    psum x3, blocking collectives, per_device(): lax.psum(gram_of(backward), ('row', 'col'))  339 us
    psum x3, blocking collectives, per_device(): lax.psum(gram_of(forward), ('row', 'col'))  306 us
    all_gather x3, blocking collectives, per_device(): user_full = lax.all_gather(scaled, 'col', axis=1, tiled=True)  170 us
    psum x1, blocking collectives, per_device(): start_total = lax.psum(gram_of(start_panel), ('row', 'col'))  111 us
    all_gather x3, blocking collectives, per_device(): item_full = lax.all_gather(scaled, 'row', axis=1, tiled=True)  107 us
    another operation x8, other arithmetic, solve_lower(): lax.linalg.triangular_solve(factor, vectors, left_side=True, lower=True)  34.9 us
  transfers between devices with their start and end apart: 6, of which 6 were waited for; matrix products, arithmetic and copies ran while one was open for 0% of the time, Pallas kernels for 0%

commit v1 on v0

--- a/solution.py
+++ b/solution.py
@@ -42,7 +42,7 @@
     item_offset = lax.axis_index("row") * item_group
     user_scale_own = lax.dynamic_slice_in_dim(user_scale, user_offset, user_group)
     item_scale_own = lax.dynamic_slice_in_dim(item_scale, item_offset, item_group)
-    start_total = lax.psum(gram_of(start_panel), ("row", "col"))
+    start_total = lax.psum(lax.psum(gram_of(start_panel), axis_name="col"), axis_name="row")
     start_factor = jnp.linalg.cholesky(start_total)
     item_basis = solve_lower(start_factor, start_panel)
     user_basis = start_panel[:, :0]

time: 1740 us -> 1880 us (1.080)
  blocking collectives: 1030 us -> 1160 us
    psum x1 -> x2, blocking collectives: 111 us -> 237 us  [the longest x1 173 us: per_device(): lax.psum(gram_of(start_panel), axis_name='col')]
where the time goes in v1:
time: 1880 us; the launch traced here: 1870 us
  blocking collectives  1160 us (62%)
  waiting for transfers between devices  562 us (30%)
  other arithmetic  87.5 us (5%)
  matrix products  25.6 us (1%)
  local copies, waits for them, and re-layouts  20.4 us (1%)
    unnamed x12, waiting for transfers between devices  562 us
    psum x3, blocking collectives, per_device(): lax.psum(gram_of(backward), ('row', 'col'))  338 us
    psum x3, blocking collectives, per_device(): lax.psum(gram_of(forward), ('row', 'col'))  306 us
    psum x1, blocking collectives, per_device(): lax.psum(gram_of(start_panel), axis_name='col')  173 us
    all_gather x3, blocking collectives, per_device(): user_full = lax.all_gather(scaled, 'col', axis=1, tiled=True)  170 us
    all_gather x3, blocking collectives, per_device(): item_full = lax.all_gather(scaled, 'row', axis=1, tiled=True)  106 us
    psum x1, blocking collectives, per_device(): lax.psum(lax.psum(gram_of(start_panel), axis_name='col'), axis_name='row')  64.7 us
  transfers between devices with their start and end apart: 6, of which 6 were waited for; matrix products, arithmetic and copies ran while one was open for 0% of the time, Pallas kernels for 0%

profile of v1, /device:TPU:1, one launch (start us, length us, event | category | flops | bytes accessed | tf_op | source)
XLA Modules:
  0.0 1868.4 jit_solution(11363802105866357653)
XLA Ops:
  9.7 172.7 %psum.56 = f32[64,64]{0,1:T(8,128)S(1)} all-reduce(f32[64,64]{0,1:T(8,128)S(1)} %fusion.153), channel_id=1, replica_groups=mesh['row'=16,'col'=32] {'col'}, use_global_device_ids=true, to_apply=%region_0.1 | all-reduce | flops 4096 | bytes 32768 | tf_op jit(solution)/shard_map/psum | solution.py:45
  182.4 64.7 %psum.57 = f32[64,64]{0,1:T(8,128)S(1)} all-reduce(f32[64,64]{0,1:T(8,128)S(1)} %psum.56), channel_id=1, replica_groups=mesh['row'=16,'col'=32] {'row'}, use_global_device_ids=true, to_apply=%region_1.2 | all-reduce | flops 4096 | bytes 32768 | tf_op jit(solution)/shard_map/psum | solution.py:45
  247.2 5.8 cholesky.119
  254.4 4.9 custom-call.13
  260.3 32.5 %all-gather = f32[16,96,64]{1,2,0:T(8,128)S(1)} all-gather(f32[1,96,64]{1,2,0:T(8,128)S(1)} %multiply_bitcast_fusion.2), channel_id=1, replica_groups=mesh['row'=16,'col'=32] {'row'}, dimensions={0}, use_global_device_ids=true | all-gather | bytes 417792 | tf_op jit(solution)/shard_map/all_gather | solution.py:54
  299.6 126.7 %reduce-scatter.19.cloned.1.call-done = f32[64,64]{1,0:T(8,128)} async-done(((f32[2048,64]{1,0:T(8,128)}), f32[64,64]{1,0:T(8,128)}) %reduce-scatter.19.cloned.1.call-update) | async-done | bytes 16400
  427.3 101.9 %psum.58 = f32[64,64]{0,1:T(8,128)S(1)} all-reduce(f32[64,64]{0,1:T(8,128)S(1)} %fusion.81), channel_id=1, replica_groups=mesh['row'=16,'col'=32] {'row','col'}, use_global_device_ids=true, to_apply=%region_5.9 | all-reduce | flops 4096 | bytes 32768 | tf_op jit(solution)/shard_map/psum | solution.py:74
  529.2 5.8 cholesky.130
  536.4 4.9 custom-call.14
  541.7 56.8 %all_gather.19 = f32[64,2048]{0,1:T(8,128)S(1)} all-gather(f32[64,64]{0,1:T(8,128)S(1)} %copy.109), channel_id=1, replica_groups=mesh['row'=16,'col'=32] {'col'}, dimensions={1}, use_global_device_ids=true | all-gather | bytes 540672 | tf_op jit(solution)/shard_map/all_gather | solution.py:77
  602.7 72.3 %reduce-scatter.21.cloned.1.call-done = f32[96,64]{1,0:T(8,128)} async-done(((f32[1536,64]{1,0:T(8,128)}), f32[96,64]{1,0:T(8,128)}) %reduce-scatter.21.cloned.1.call-update) | async-done | bytes 24592
  677.0 112.7 %psum.59 = f32[64,64]{0,1:T(8,128)S(1)} all-reduce(f32[64,64]{0,1:T(8,128)S(1)} %fusion.154), channel_id=1, replica_groups=mesh['row'=16,'col'=32] {'row','col'}, use_global_device_ids=true, to_apply=%region_7.13 | all-reduce | flops 4096 | bytes 32768 | tf_op jit(solution)/shard_map/psum | solution.py:92
  789.8 5.8 cholesky.141
  797.0 4.9 custom-call.15
  802.2 36.3 %all-gather.1 = f32[16,96,64]{1,2,0:T(8,128)S(1)} all-gather(f32[1,96,64]{1,2,0:T(8,128)S(1)} %multiply_bitcast_fusion.1), channel_id=1, replica_groups=mesh['row'=16,'col'=32] {'row'}, dimensions={0}, use_global_device_ids=true | all-gather | bytes 417792 | tf_op jit(solution)/shard_map/all_gather | solution.py:54
  844.4 110.1 %reduce-scatter.23.cloned.1.call-done = f32[64,64]{1,0:T(8,128)} async-done(((f32[2048,64]{1,0:T(8,128)}), f32[64,64]{1,0:T(8,128)}) %reduce-scatter.23.cloned.1.call-update) | async-done | bytes 16400
  956.4 102.0 %psum.60 = f32[64,64]{0,1:T(8,128)S(1)} all-reduce(f32[64,64]{0,1:T(8,128)S(1)} %fusion.155), channel_id=1, replica_groups=mesh['row'=16,'col'=32] {'row','col'}, use_global_device_ids=true, to_apply=%region_9.15 | all-reduce | flops 4096 | bytes 32768 | tf_op jit(solution)/shard_map/psum | solution.py:74
  1058.5 5.8 cholesky.152
  1070.9 57.0 %all_gather.21 = f32[64,2048]{0,1:T(8,128)S(1)} all-gather(f32[64,64]{0,1:T(8,128)S(1)} %copy.120), channel_id=1, replica_groups=mesh['row'=16,'col'=32] {'col'}, dimensions={1}, use_global_device_ids=true | all-gather | bytes 540672 | tf_op jit(solution)/shard_map/all_gather | solution.py:77
  1132.2 70.9 %reduce-scatter.25.cloned.1.call-done = f32[96,64]{1,0:T(8,128)} async-done(((f32[1536,64]{1,0:T(8,128)}), f32[96,64]{1,0:T(8,128)}) %reduce-scatter.25.cloned.1.call-update) | async-done | bytes 24592
  1205.0 112.6 %psum.61 = f32[64,64]{0,1:T(8,128)S(1)} all-reduce(f32[64,64]{0,1:T(8,128)S(1)} %fusion.156), channel_id=1, replica_groups=mesh['row'=16,'col'=32] {'row','col'}, use_global_device_ids=true, to_apply=%region_11.17 | all-reduce | flops 4096 | bytes 32768 | tf_op jit(solution)/shard_map/psum | solution.py:92
  1317.8 5.8 cholesky.163
  1330.1 36.7 %all-gather.2 = f32[16,96,64]{1,2,0:T(8,128)S(1)} all-gather(f32[1,96,64]{1,2,0:T(8,128)S(1)} %multiply_bitcast_fusion), channel_id=1, replica_groups=mesh['row'=16,'col'=32] {'row'}, dimensions={0}, use_global_device_ids=true | all-gather | bytes 417792 | tf_op jit(solution)/shard_map/all_gather | solution.py:54
  1372.7 110.1 %reduce-scatter.27.cloned.1.call-done = f32[64,64]{1,0:T(8,128)} async-done(((f32[2048,64]{1,0:T(8,128)}), f32[64,64]{1,0:T(8,128)}) %reduce-scatter.27.cloned.1.call-update) | async-done | bytes 16400
  1484.7 101.8 %psum.62 = f32[64,64]{0,1:T(8,128)S(1)} all-reduce(f32[64,64]{0,1:T(8,128)S(1)} %fusion.157), channel_id=1, replica_groups=mesh['row'=16,'col'=32] {'row','col'}, use_global_device_ids=true, to_apply=%region_13.19 | all-reduce | flops 4096 | bytes 32768 | tf_op jit(solution)/shard_map/psum | solution.py:74
  1586.6 5.8 cholesky.174
  1593.8 4.9 custom-call.18
  1599.7 56.3 %all_gather.23 = f32[64,2048]{0,1:T(8,128)S(1)} all-gather(f32[64,64]{0,1:T(8,128)S(1)} %copy.131), channel_id=1, replica_groups=mesh['row'=16,'col'=32] {'col'}, dimensions={1}, use_global_device_ids=true | all-gather | bytes 540672 | tf_op jit(solution)/shard_map/all_gather | solution.py:77
  1660.9 71.7 %reduce-scatter.29.cloned.1.call-done = f32[96,64]{1,0:T(8,128)} async-done(((f32[1536,64]{1,0:T(8,128)}), f32[96,64]{1,0:T(8,128)}) %reduce-scatter.29.cloned.1.call-update) | async-done | bytes 24592
  1734.5 113.0 %psum.63 = f32[64,64]{0,1:T(8,128)S(1)} all-reduce(f32[64,64]{0,1:T(8,128)S(1)} %fusion.158), channel_id=1, replica_groups=mesh['row'=16,'col'=32] {'row','col'}, use_global_device_ids=true, to_apply=%region_15.21 | all-reduce | flops 4096 | bytes 32768 | tf_op jit(solution)/shard_map/psum | solution.py:92
  1847.7 5.8 cholesky.185
  1854.8 4.9 custom-call.19
  (131 shorter events, 68.4 us)
Async XLA Ops:
  7.2 286.9 %copy-start = (bf16[1,1,32,128,128]{4,3,2,1,0:T(8,128)(2,1)S(1)}, bf16[1,1,32,128,128]{4,3,2,1,0:T(8,128)(2,1)}, u32[]{:S(2)}) copy-start(bf16[1,1,32,128,128]{4,3,2,1,0:T(8,128)(2,1)} %param.15) | copy-start | bytes 3145732
  7.2 419.1 %reduce-scatter.19.cloned.1.call-start = ((), (), s32[]{:S(2)}) async-start(), calls=%async_computation.6 | async-start | bytes 1081344
  8.0 0.7 copy-start.2
  253.7 5.6 copy-start.1
  298.7 376.3 %reduce-scatter.21.cloned.1.call-start = ((), (), s32[]{:S(2)}) async-start(), calls=%async_computation.7 | async-start | bytes 835584
  602.7 351.8 %reduce-scatter.23.cloned.1.call-start = ((), (), s32[]{:S(2)}) async-start(), calls=%async_computation.8 | async-start | bytes 1081344
  844.3 358.7 %reduce-scatter.25.cloned.1.call-start = ((), (), s32[]{:S(2)}) async-start(), calls=%async_computation.9 | async-start | bytes 835584
  1132.1 350.7 %reduce-scatter.27.cloned.1.call-start = ((), (), s32[]{:S(2)}) async-start(), calls=%async_computation.10 | async-start | bytes 1081344
  1372.6 359.9 %reduce-scatter.29.cloned.1.call-start = ((), (), s32[]{:S(2)}) async-start(), calls=%async_computation.11 | async-start | bytes 835584
Sparse Core Ops, SparseCore 0:
  298.9 127.3 reduce-scatter.18
  602.8 72.1 reduce-scatter.20
  844.5 109.9 reduce-scatter.22
  1132.2 70.7 reduce-scatter.24
  1372.8 110.0 reduce-scatter.26
  1660.3 72.1 reduce-scatter.28
